TPU v7x, 128 devices: a whole 4x4x4 slice. The times are simulated.
128 devices in a mesh: dom: 16 (over y_lo, z, core), rep: 8 (over y_hi, x).
Axes of the slice: x: 4, y: 4 (y_hi: 2, y_lo: 2; y = y_hi * 2 + y_lo), z: 4, core: 2. Of those that a mesh axis runs over, the one named last changes fastest.
Arguments:
- node_features: bfloat16 [65536, 256], P(('dom', 'rep')), may hold values from -6 to 6
- weight: bfloat16 [256, 256], replicated, may hold values from -0.375 to 0.375
- cotangent: bfloat16 [65536, 256], P(('dom', 'rep')), may hold values from -6 to 6
- tile_row: int32 [16, 8, 512], P('dom', 'rep'), may hold values from 0 to 31
- tile_col: int32 [16, 8, 512], P('dom', 'rep'), may hold values from 0 to 63
- tile_values: bfloat16 [16, 8, 512, 128, 128], P('dom', 'rep'), may hold values from -0.0625 to 0.0625
- tile_count: int32 [16, 8], P('dom', 'rep'), may hold values from 128 to 512, as said below
Outputs:
- output: bfloat16 [65536, 256], P(('dom', 'rep'))
- grad_features: bfloat16 [65536, 256], P(('dom', 'rep'))
- grad_weight: float32 [256, 256], replicated
Inputs may be any that keep to these rules, and one draw needn't show every extreme that they name: Live slots are the first tile_count slots of each device's list; some device has all 512 slots live.
All inputs are finite; a program needn't handle non-finite values.
Results may differ from a plain program's by a relative error of at most 0.0061.
Values may be sent and summed in bfloat16 or wider, within the bound.
No kernel may reach another device: no remote copies, remote signals or barrier semaphores. Data moves between devices by JAX's collectives and lax.ppermute only.
A program may use at most 192 MiB of HBM per device.

v0:
```python
import jax
import jax.numpy as jnp
from jax import lax
from jax.sharding import PartitionSpec as P


def silu_slope(summed):
    sig = jax.nn.sigmoid(summed)
    return sig * (1.0 + summed * (1.0 - sig))


def tile_products(values, pick_index, place_index, active, source, out_blocks, flipped):
    slots = values.shape[0]
    feature_width = source.shape[2]
    per_turn = min(slots, 128)
    pattern = "tba,tbf->taf" if flipped else "tab,tbf->taf"

    def accumulate(turn_index, summed):
        first_slot = turn_index * per_turn
        block_values = lax.dynamic_slice_in_dim(values, first_slot, per_turn, 0)
        picks = lax.dynamic_slice_in_dim(pick_index, first_slot, per_turn, 0)
        picked = jnp.take(source, picks, axis=0)
        products = jnp.einsum(pattern, block_values, picked, preferred_element_type=jnp.float32)
        places = lax.dynamic_slice_in_dim(place_index, first_slot, per_turn, 0)
        enabled = lax.dynamic_slice_in_dim(active, first_slot, per_turn, 0)
        products = products * enabled.astype(jnp.float32)[:, None, None]
        return summed.at[places].add(products)

    initial = jnp.zeros((out_blocks, 128, feature_width), jnp.float32)
    summed = lax.fori_loop(0, slots // per_turn, accumulate, initial)
    return summed.reshape(out_blocks * 128, feature_width)


def body(node_features, weight, cotangent, tile_row, tile_col, tile_values, tile_count):
    rows_here = node_features.shape[0]
    feature_width = weight.shape[0]
    dom_size = lax.axis_size("dom")
    rep_size = lax.axis_size("rep")
    slots = tile_row.shape[2]
    row_index = tile_row.reshape(slots)
    col_index = tile_col.reshape(slots)
    values = tile_values.reshape(slots, 128, 128)
    active = lax.broadcasted_iota(jnp.int32, (slots,), 0) < tile_count.reshape(())
    projected = jnp.dot(node_features, weight, preferred_element_type=jnp.float32).astype(
        jnp.bfloat16
    )
    gathered = lax.all_gather(projected, "dom", axis=0, tiled=True)
    source = gathered.reshape(-1, 128, feature_width)
    part_blocks = rep_size * rows_here // 128
    partial_value = tile_products(values, col_index, row_index, active, source, part_blocks, False)
    summed = lax.psum_scatter(partial_value, "rep", scatter_dimension=0, tiled=True)
    output = jax.nn.silu(summed).astype(jnp.bfloat16)
    grad_own = (cotangent.astype(jnp.float32) * silu_slope(summed)).astype(jnp.bfloat16)
    grad_block = lax.all_gather(grad_own, "rep", axis=0, tiled=True)
    back_blocks = dom_size * rows_here // 128
    back_partial = tile_products(
        values,
        row_index,
        col_index,
        active,
        grad_block.reshape(-1, 128, feature_width),
        back_blocks,
        True,
    )
    grad_projected = lax.psum_scatter(back_partial, "dom", scatter_dimension=0, tiled=True).astype(
        jnp.bfloat16
    )
    grad_features = jnp.dot(grad_projected, weight.T, preferred_element_type=jnp.float32).astype(
        jnp.bfloat16
    )
    local_weight = jnp.dot(node_features.T, grad_projected, preferred_element_type=jnp.float32)
    grad_weight = lax.psum(local_weight, ("dom", "rep"))
    return (output, grad_features, grad_weight)


def solution(mesh):
    placed = (
        P(("dom", "rep"), None),
        P(),
        P(("dom", "rep"), None),
        P("dom", "rep", None),
        P("dom", "rep", None),
        P("dom", "rep", None, None, None),
        P("dom", "rep"),
    )
    return jax.shard_map(
        body,
        mesh=mesh,
        in_specs=placed,
        out_specs=(P(("dom", "rep"), None), P(("dom", "rep"), None), P()),
        check_vma=False,
    )
```

profile of v0, /device:TPU:1, one launch (start us, length us, event | category | flops | bytes accessed | tf_op | source)
XLA Modules:
  0.0 908.0 jit_solution(10777865380881318707)
XLA Ops:
  10.7 40.7 %all-gather.3.cloned.1.call-done = bf16[8192,256]{1,0:T(8,128)(2,1)} async-done(((bf16[512,256]{1,0:T(8,128)(2,1)}), bf16[8192,256]{1,0:T(8,128)(2,1)}) %all-gather.3.cloned.1.call-update) | async-done | bytes 4194320 | tf_op jit(solution)/shard_map/all_gather | solution.py:47
  53.8 244.2 %while.26 = (s32[]{:T(128)}, f32[32,128,256]{2,1,0:T(8,128)}, s32[512]{0:T(512)}, bf16[512,128,128]{2,1,0:T(8,128)(2,1)}, s32[512]{0:T(512)}, /*index=5*/bf16[64...) while((s32[]{:T(128)}, f32[32,128,256]{2,1,0:T(8,128)}, ...), condition=%wide.region_2.3_spmd, body=%wide.region_0.2_spmd.sunk | while | flops 1086327040 | bytes 96478248 | solution.py:30
  63.4 12.8 %convolution_multiply_fusion.4 = f32[128,128,256]{2,1,0:T(8,128)} fusion(f32[128]{0:T(128)S(1)} %get-tuple-element.384, bf16[128,128,256]{2,1,0:T(8,128)(2,1)} %gather_fusion, pred[128]{0:T(512)(128)(4,1)S(1)} %get-tuple-element.386, bf16[512,128,128]{2,1,0:T(8,128)(2,1)} %get-tuple-element.422, s32[]{:T(128)S(6)} %select_n.85), kind=kOutput, calls=%fused_computation.4.clone.1 | convolution fusion | flops 1082130432 | bytes 29360772 | tf_op jit(solution)/shard_map/while/body/eval_jaxpr/tab,tbf->taf/dot_general | solution.py:23
  76.9 38.1 %scatter_fusion = f32[32,128,256]{2,1,0:T(8,128)} fusion(f32[32,128,256]{2,1,0:T(8,128)} %get-tuple-element.409, s32[128]{0:T(128)S(1)} %compare_select_fusion.8, f32[128,128,256]{2,1,0:T(8,128)} %convolution_multiply_fusion.4), kind=kCustom, calls=%fused_computation.2.clone.1 | custom fusion | flops 4194304 | bytes 50332160 | tf_op jit(solution)/shard_map/while/body/eval_jaxpr/scatter-add | solution.py:27
  124.5 12.8 %convolution_multiply_fusion.4 = f32[128,128,256]{2,1,0:T(8,128)} fusion(f32[128]{0:T(128)S(1)} %get-tuple-element.384, bf16[128,128,256]{2,1,0:T(8,128)(2,1)} %gather_fusion, pred[128]{0:T(512)(128)(4,1)S(1)} %get-tuple-element.386, bf16[512,128,128]{2,1,0:T(8,128)(2,1)} %get-tuple-element.422, s32[]{:T(128)S(6)} %select_n.85), kind=kOutput, calls=%fused_computation.4.clone.1 | convolution fusion | flops 1082130432 | bytes 29360772 | tf_op jit(solution)/shard_map/while/body/eval_jaxpr/tab,tbf->taf/dot_general | solution.py:23
  138.1 38.1 %scatter_fusion = f32[32,128,256]{2,1,0:T(8,128)} fusion(f32[32,128,256]{2,1,0:T(8,128)} %get-tuple-element.409, s32[128]{0:T(128)S(1)} %compare_select_fusion.8, f32[128,128,256]{2,1,0:T(8,128)} %convolution_multiply_fusion.4), kind=kCustom, calls=%fused_computation.2.clone.1 | custom fusion | flops 4194304 | bytes 50332160 | tf_op jit(solution)/shard_map/while/body/eval_jaxpr/scatter-add | solution.py:27
  185.7 12.8 %convolution_multiply_fusion.4 = f32[128,128,256]{2,1,0:T(8,128)} fusion(f32[128]{0:T(128)S(1)} %get-tuple-element.384, bf16[128,128,256]{2,1,0:T(8,128)(2,1)} %gather_fusion, pred[128]{0:T(512)(128)(4,1)S(1)} %get-tuple-element.386, bf16[512,128,128]{2,1,0:T(8,128)(2,1)} %get-tuple-element.422, s32[]{:T(128)S(6)} %select_n.85), kind=kOutput, calls=%fused_computation.4.clone.1 | convolution fusion | flops 1082130432 | bytes 29360772 | tf_op jit(solution)/shard_map/while/body/eval_jaxpr/tab,tbf->taf/dot_general | solution.py:23
  199.3 37.7 %scatter_fusion = f32[32,128,256]{2,1,0:T(8,128)} fusion(f32[32,128,256]{2,1,0:T(8,128)} %get-tuple-element.409, s32[128]{0:T(128)S(1)} %compare_select_fusion.8, f32[128,128,256]{2,1,0:T(8,128)} %convolution_multiply_fusion.4), kind=kCustom, calls=%fused_computation.2.clone.1 | custom fusion | flops 4194304 | bytes 50332160 | tf_op jit(solution)/shard_map/while/body/eval_jaxpr/scatter-add | solution.py:27
  246.5 12.8 %convolution_multiply_fusion.4 = f32[128,128,256]{2,1,0:T(8,128)} fusion(f32[128]{0:T(128)S(1)} %get-tuple-element.384, bf16[128,128,256]{2,1,0:T(8,128)(2,1)} %gather_fusion, pred[128]{0:T(512)(128)(4,1)S(1)} %get-tuple-element.386, bf16[512,128,128]{2,1,0:T(8,128)(2,1)} %get-tuple-element.422, s32[]{:T(128)S(6)} %select_n.85), kind=kOutput, calls=%fused_computation.4.clone.1 | convolution fusion | flops 1082130432 | bytes 29360772 | tf_op jit(solution)/shard_map/while/body/eval_jaxpr/tab,tbf->taf/dot_general | solution.py:23
  260.1 37.9 %scatter_fusion = f32[32,128,256]{2,1,0:T(8,128)} fusion(f32[32,128,256]{2,1,0:T(8,128)} %get-tuple-element.409, s32[128]{0:T(128)S(1)} %compare_select_fusion.8, f32[128,128,256]{2,1,0:T(8,128)} %convolution_multiply_fusion.4), kind=kCustom, calls=%fused_computation.2.clone.1 | custom fusion | flops 4194304 | bytes 50332160 | tf_op jit(solution)/shard_map/while/body/eval_jaxpr/scatter-add | solution.py:27
  298.0 83.2 %reduce-scatter.3.cloned.1.call-done = f32[512,256]{1,0:T(8,128)} async-done(((f32[4096,256]{1,0:T(8,128)}), f32[512,256]{1,0:T(8,128)}) %reduce-scatter.3.cloned.1.call-update) | async-done | bytes 524304 | tf_op jit(solution)/shard_map/reduce_scatter | solution.py:51
  383.6 22.4 %copy.10 = bf16[1,1,512,128,128]{3,4,2,1,0:T(8,128)(2,1)} copy(bf16[1,1,512,128,128]{4,3,2,1,0:T(8,128)(2,1)} %bitcast.21) | data formatting | bytes 33554432 | tf_op args[5]
  406.0 31.9 %all-gather.5.cloned.1.call-done = bf16[4096,256]{1,0:T(8,128)(2,1)} async-done(((bf16[512,256]{1,0:T(8,128)(2,1)}), bf16[4096,256]{1,0:T(8,128)(2,1)}) %all-gather.5.cloned.1.call-update) | async-done | bytes 2097168 | tf_op jit(solution)/shard_map/all_gather | solution.py:54
  442.1 236.8 %while.27 = (s32[]{:T(128)}, f32[64,128,256]{2,1,0:T(8,128)}, s32[512]{0:T(512)}, bf16[512,128,128]{1,2,0:T(8,128)(2,1)}, s32[512]{0:T(512)}, /*index=5*/bf16[32...) while((s32[]{:T(128)}, f32[64,128,256]{2,1,0:T(8,128)}, ...), condition=%wide.region_6.7_spmd, body=%wide.region_4.6_spmd.sunk | while | flops 1086327040 | bytes 96478248 | solution.py:30
  449.5 12.8 %convolution_multiply_fusion.5 = f32[128,128,256]{2,1,0:T(8,128)} fusion(f32[128]{0:T(128)S(1)} %get-tuple-element.394, bf16[128,128,256]{2,1,0:T(8,128)(2,1)} %gather_fusion.1, pred[128]{0:T(512)(128)(4,1)S(1)} %get-tuple-element.396, bf16[512,128,128]{1,2,0:T(8,128)(2,1)} %get-tuple-element.455, s32[]{:T(128)S(6)} %select_n.88), kind=kOutput, calls=%fused_computation.16.clone.1 | convolution fusion | flops 1082130432 | bytes 29360772 | tf_op jit(solution)/shard_map/while/body/eval_jaxpr/tba,tbf->taf/dot_general | solution.py:23
  463.1 38.5 %scatter_fusion.1 = f32[64,128,256]{2,1,0:T(8,128)} fusion(f32[64,128,256]{2,1,0:T(8,128)} %get-tuple-element.442, s32[128]{0:T(128)S(1)} %compare_select_fusion.9, f32[128,128,256]{2,1,0:T(8,128)} %convolution_multiply_fusion.5), kind=kCustom, calls=%fused_computation.3.clone.1 | custom fusion | flops 4194304 | bytes 50332160 | tf_op jit(solution)/shard_map/while/body/eval_jaxpr/scatter-add | solution.py:27
  508.9 12.8 %convolution_multiply_fusion.5 = f32[128,128,256]{2,1,0:T(8,128)} fusion(f32[128]{0:T(128)S(1)} %get-tuple-element.394, bf16[128,128,256]{2,1,0:T(8,128)(2,1)} %gather_fusion.1, pred[128]{0:T(512)(128)(4,1)S(1)} %get-tuple-element.396, bf16[512,128,128]{1,2,0:T(8,128)(2,1)} %get-tuple-element.455, s32[]{:T(128)S(6)} %select_n.88), kind=kOutput, calls=%fused_computation.16.clone.1 | convolution fusion | flops 1082130432 | bytes 29360772 | tf_op jit(solution)/shard_map/while/body/eval_jaxpr/tba,tbf->taf/dot_general | solution.py:23
  522.5 38.1 %scatter_fusion.1 = f32[64,128,256]{2,1,0:T(8,128)} fusion(f32[64,128,256]{2,1,0:T(8,128)} %get-tuple-element.442, s32[128]{0:T(128)S(1)} %compare_select_fusion.9, f32[128,128,256]{2,1,0:T(8,128)} %convolution_multiply_fusion.5), kind=kCustom, calls=%fused_computation.3.clone.1 | custom fusion | flops 4194304 | bytes 50332160 | tf_op jit(solution)/shard_map/while/body/eval_jaxpr/scatter-add | solution.py:27
  567.9 12.8 %convolution_multiply_fusion.5 = f32[128,128,256]{2,1,0:T(8,128)} fusion(f32[128]{0:T(128)S(1)} %get-tuple-element.394, bf16[128,128,256]{2,1,0:T(8,128)(2,1)} %gather_fusion.1, pred[128]{0:T(512)(128)(4,1)S(1)} %get-tuple-element.396, bf16[512,128,128]{1,2,0:T(8,128)(2,1)} %get-tuple-element.455, s32[]{:T(128)S(6)} %select_n.88), kind=kOutput, calls=%fused_computation.16.clone.1 | convolution fusion | flops 1082130432 | bytes 29360772 | tf_op jit(solution)/shard_map/while/body/eval_jaxpr/tba,tbf->taf/dot_general | solution.py:23
  581.5 38.3 %scatter_fusion.1 = f32[64,128,256]{2,1,0:T(8,128)} fusion(f32[64,128,256]{2,1,0:T(8,128)} %get-tuple-element.442, s32[128]{0:T(128)S(1)} %compare_select_fusion.9, f32[128,128,256]{2,1,0:T(8,128)} %convolution_multiply_fusion.5), kind=kCustom, calls=%fused_computation.3.clone.1 | custom fusion | flops 4194304 | bytes 50332160 | tf_op jit(solution)/shard_map/while/body/eval_jaxpr/scatter-add | solution.py:27
  627.1 12.8 %convolution_multiply_fusion.5 = f32[128,128,256]{2,1,0:T(8,128)} fusion(f32[128]{0:T(128)S(1)} %get-tuple-element.394, bf16[128,128,256]{2,1,0:T(8,128)(2,1)} %gather_fusion.1, pred[128]{0:T(512)(128)(4,1)S(1)} %get-tuple-element.396, bf16[512,128,128]{1,2,0:T(8,128)(2,1)} %get-tuple-element.455, s32[]{:T(128)S(6)} %select_n.88), kind=kOutput, calls=%fused_computation.16.clone.1 | convolution fusion | flops 1082130432 | bytes 29360772 | tf_op jit(solution)/shard_map/while/body/eval_jaxpr/tba,tbf->taf/dot_general | solution.py:23
  640.7 38.3 %scatter_fusion.1 = f32[64,128,256]{2,1,0:T(8,128)} fusion(f32[64,128,256]{2,1,0:T(8,128)} %get-tuple-element.442, s32[128]{0:T(128)S(1)} %compare_select_fusion.9, f32[128,128,256]{2,1,0:T(8,128)} %convolution_multiply_fusion.5), kind=kCustom, calls=%fused_computation.3.clone.1 | custom fusion | flops 4194304 | bytes 50332160 | tf_op jit(solution)/shard_map/while/body/eval_jaxpr/scatter-add | solution.py:27
  679.0 71.8 %reduce-scatter.5.cloned.1.call-done = f32[512,256]{1,0:T(8,128)} async-done(((f32[8192,256]{1,0:T(8,128)}), f32[512,256]{1,0:T(8,128)}) %reduce-scatter.5.cloned.1.call-update) | async-done | bytes 524304 | tf_op jit(solution)/shard_map/reduce_scatter | solution.py:65
  754.9 144.8 %all-reduce.2.cloned.1.call-done = f32[256,256]{0,1:T(8,128)} async-done(((f32[256,256]{0,1:T(8,128)}), f32[256,256]{0,1:T(8,128)}) %all-reduce.2.cloned.1.call-update) | async-done | bytes 262160 | tf_op jit(solution)/shard_map/psum | solution.py:72
  (58 shorter events, 91.3 us)
Async XLA Ops:
  7.2 1.0 copy-start
  7.2 44.2 %all-gather.3.cloned.1.call-start = ((), (), s32[]{:S(2)}) async-start(), calls=%async_computation.2 | async-start | bytes 4456448 | tf_op jit(solution)/shard_map/all_gather | solution.py:47
  10.0 371.3 %reduce-scatter.3.cloned.1.call-start = ((), (), s32[]{:S(2)}) async-start(), calls=%async_computation.3 | async-start | bytes 4718592 | tf_op jit(solution)/shard_map/reduce_scatter | solution.py:51
  53.8 327.5 %copy-start.3 = (bf16[512,256]{1,0:T(8,128)(2,1)S(1)}, bf16[512,256]{1,0:T(8,128)(2,1)}, u32[]{:S(2)}) copy-start(bf16[512,256]{1,0:T(8,128)(2,1)} %param.13) | copy-start | bytes 786436
  298.0 139.9 %all-gather.5.cloned.1.call-start = ((), (), s32[]{:S(2)}) async-start(), calls=%async_computation.4 | async-start | bytes 2359296 | tf_op jit(solution)/shard_map/all_gather | solution.py:54
  383.4 367.4 %reduce-scatter.5.cloned.1.call-start = ((), (), s32[]{:S(2)}) async-start(), calls=%async_computation.5 | async-start | bytes 8912896 | tf_op jit(solution)/shard_map/reduce_scatter | solution.py:65
  437.9 4.2 copy-start.1
  679.0 73.9 %copy-start.2 = (bf16[256,256]{1,0:T(8,128)(2,1)S(1)}, bf16[256,256]{1,0:T(8,128)(2,1)}, u32[]{:S(2)}) copy-start(bf16[256,256]{1,0:T(8,128)(2,1)} %param.12) | copy-start | bytes 393220
  679.0 220.6 %all-reduce.2.cloned.1.call-start = ((), (), s32[]{:S(2)}) async-start(), calls=%async_computation.6 | async-start | bytes 524288 | tf_op jit(solution)/shard_map/psum | solution.py:72
Sparse Core Ops, SparseCore 0:
  10.3 41.0 all-gather.2
  298.1 83.1 reduce-scatter.2
  384.2 53.6 all-gather.4
  679.1 71.6 reduce-scatter.4
  756.0 143.6 all-reduce.1
where the time goes:
time: 910 us; the launch traced here: 908 us
  waiting for transfers between devices  372 us (41%)
  other arithmetic  319 us (35%)
  matrix products  108 us (12%)
  local copies, waits for them, and re-layouts  93.1 us (10%)
  between operations  14.5 us (2%)
    scatter-add x8, other arithmetic, accumulate(): return summed.at[places].add(products)  305 us
    psum x1, waiting for transfers between devices, body(): grad_weight = lax.psum(local_weight, ('dom', 'rep'))  145 us
    dot_general x8, matrix products, accumulate(): jnp.einsum(pattern, block_values, picked, preferred_element_type=jnp.floa...  103 us
    reduce_scatter x1, waiting for transfers between devices, body(): lax.psum_scatter(partial_value, 'rep', scatter_dimension=0, tiled=True)  83.2 us
    reduce_scatter x1, waiting for transfers between devices, body(): lax.psum_scatter(back_partial, 'dom', scatter_dimension=0, tiled=True)  71.8 us
    gather x8, local copies, waits for them, and re-layouts, accumulate(): picked = jnp.take(source, picks, axis=0)  61.3 us
    all_gather x1, waiting for transfers between devices, body(): gathered = lax.all_gather(projected, 'dom', axis=0, tiled=True)  40.7 us
    all_gather x1, waiting for transfers between devices, body(): grad_block = lax.all_gather(grad_own, 'rep', axis=0, tiled=True)  31.9 us
  transfers between devices with their start and end apart: 5, of which 5 were waited for; matrix products, arithmetic and copies ran while one was open for 3% of the time, Pallas kernels for 0%

commit v1 on v0

--- a/solution.py
+++ b/solution.py
@@ -2,6 +2,7 @@
 import jax.numpy as jnp
 from jax import lax
 from jax.sharding import PartitionSpec as P
+from jax.lax import psum
 
 
 def silu_slope(summed):
@@ -69,7 +70,7 @@
         jnp.bfloat16
     )
     local_weight = jnp.dot(node_features.T, grad_projected, preferred_element_type=jnp.float32)
-    grad_weight = lax.psum(local_weight, ("dom", "rep"))
+    grad_weight = psum(psum(local_weight, axis_name="dom"), axis_name="rep")
     return (output, grad_features, grad_weight)
 
 

time: 910 us -> 970 us (1.066)
  waiting for transfers between devices: 372 us -> 428 us
    psum x1 -> x2, waiting for transfers between devices: 145 us -> 200 us  [body(): grad_weight = psum(psum(local_weight, axis_name='dom'), axis_name='rep')]
  transfers between devices with their start and end apart: 5 -> 6, of which waited for: 5 -> 6; matrix products, arithmetic and copies ran while one was open for 3% -> 3% of each run, Pallas kernels for 0% -> 0%
where the time goes in v1:
time: 970 us; the launch traced here: 964 us
  waiting for transfers between devices  428 us (44%)
  other arithmetic  319 us (33%)
  matrix products  108 us (11%)
  local copies, waits for them, and re-layouts  93.1 us (10%)
  between operations  14.8 us (2%)
    scatter-add x8, other arithmetic, accumulate(): return summed.at[places].add(products)  305 us
    psum x2, waiting for transfers between devices, body(): grad_weight = psum(psum(local_weight, axis_name='dom'), axis_name='rep')  200 us
    dot_general x8, matrix products, accumulate(): jnp.einsum(pattern, block_values, picked, preferred_element_type=jnp.floa...  103 us
    reduce_scatter x1, waiting for transfers between devices, body(): lax.psum_scatter(partial_value, 'rep', scatter_dimension=0, tiled=True)  83.2 us
    reduce_scatter x1, waiting for transfers between devices, body(): lax.psum_scatter(back_partial, 'dom', scatter_dimension=0, tiled=True)  71.8 us
    gather x8, local copies, waits for them, and re-layouts, accumulate(): picked = jnp.take(source, picks, axis=0)  61.3 us
    all_gather x1, waiting for transfers between devices, body(): gathered = lax.all_gather(projected, 'dom', axis=0, tiled=True)  40.7 us
    all_gather x1, waiting for transfers between devices, body(): grad_block = lax.all_gather(grad_own, 'rep', axis=0, tiled=True)  31.9 us
  transfers between devices with their start and end apart: 6, of which 6 were waited for; matrix products, arithmetic and copies ran while one was open for 3% of the time, Pallas kernels for 0%

profile of v1, /device:TPU:1, one launch (start us, length us, event | category | flops | bytes accessed | tf_op | source)
XLA Modules:
  0.0 963.6 jit_solution(4161068462464806824)
XLA Ops:
  10.7 40.7 %all-gather.3.cloned.1.call-done = bf16[8192,256]{1,0:T(8,128)(2,1)} async-done(((bf16[512,256]{1,0:T(8,128)(2,1)}), bf16[8192,256]{1,0:T(8,128)(2,1)}) %all-gather.3.cloned.1.call-update) | async-done | bytes 4194320 | tf_op jit(solution)/shard_map/all_gather | solution.py:48
  53.8 244.2 %while.26 = (s32[]{:T(128)}, f32[32,128,256]{2,1,0:T(8,128)}, s32[512]{0:T(512)}, bf16[512,128,128]{2,1,0:T(8,128)(2,1)}, s32[512]{0:T(512)}, /*index=5*/bf16[64...) while((s32[]{:T(128)}, f32[32,128,256]{2,1,0:T(8,128)}, ...), condition=%wide.region_2.3_spmd, body=%wide.region_0.2_spmd.sunk | while | flops 1086327040 | bytes 96478248 | solution.py:31
  63.4 12.8 %convolution_multiply_fusion.4 = f32[128,128,256]{2,1,0:T(8,128)} fusion(f32[128]{0:T(128)S(1)} %get-tuple-element.384, bf16[128,128,256]{2,1,0:T(8,128)(2,1)} %gather_fusion, pred[128]{0:T(512)(128)(4,1)S(1)} %get-tuple-element.386, bf16[512,128,128]{2,1,0:T(8,128)(2,1)} %get-tuple-element.422, s32[]{:T(128)S(6)} %select_n.85), kind=kOutput, calls=%fused_computation.4.clone.1 | convolution fusion | flops 1082130432 | bytes 29360772 | tf_op jit(solution)/shard_map/while/body/eval_jaxpr/tab,tbf->taf/dot_general | solution.py:24
  76.9 38.1 %scatter_fusion = f32[32,128,256]{2,1,0:T(8,128)} fusion(f32[32,128,256]{2,1,0:T(8,128)} %get-tuple-element.409, s32[128]{0:T(128)S(1)} %compare_select_fusion.8, f32[128,128,256]{2,1,0:T(8,128)} %convolution_multiply_fusion.4), kind=kCustom, calls=%fused_computation.2.clone.1 | custom fusion | flops 4194304 | bytes 50332160 | tf_op jit(solution)/shard_map/while/body/eval_jaxpr/scatter-add | solution.py:28
  138.1 38.1 %scatter_fusion = f32[32,128,256]{2,1,0:T(8,128)} fusion(f32[32,128,256]{2,1,0:T(8,128)} %get-tuple-element.409, s32[128]{0:T(128)S(1)} %compare_select_fusion.8, f32[128,128,256]{2,1,0:T(8,128)} %convolution_multiply_fusion.4), kind=kCustom, calls=%fused_computation.2.clone.1 | custom fusion | flops 4194304 | bytes 50332160 | tf_op jit(solution)/shard_map/while/body/eval_jaxpr/scatter-add | solution.py:28
  185.7 12.8 %convolution_multiply_fusion.4 = f32[128,128,256]{2,1,0:T(8,128)} fusion(f32[128]{0:T(128)S(1)} %get-tuple-element.384, bf16[128,128,256]{2,1,0:T(8,128)(2,1)} %gather_fusion, pred[128]{0:T(512)(128)(4,1)S(1)} %get-tuple-element.386, bf16[512,128,128]{2,1,0:T(8,128)(2,1)} %get-tuple-element.422, s32[]{:T(128)S(6)} %select_n.85), kind=kOutput, calls=%fused_computation.4.clone.1 | convolution fusion | flops 1082130432 | bytes 29360772 | tf_op jit(solution)/shard_map/while/body/eval_jaxpr/tab,tbf->taf/dot_general | solution.py:24
  199.3 37.7 %scatter_fusion = f32[32,128,256]{2,1,0:T(8,128)} fusion(f32[32,128,256]{2,1,0:T(8,128)} %get-tuple-element.409, s32[128]{0:T(128)S(1)} %compare_select_fusion.8, f32[128,128,256]{2,1,0:T(8,128)} %convolution_multiply_fusion.4), kind=kCustom, calls=%fused_computation.2.clone.1 | custom fusion | flops 4194304 | bytes 50332160 | tf_op jit(solution)/shard_map/while/body/eval_jaxpr/scatter-add | solution.py:28
  246.5 12.8 %convolution_multiply_fusion.4 = f32[128,128,256]{2,1,0:T(8,128)} fusion(f32[128]{0:T(128)S(1)} %get-tuple-element.384, bf16[128,128,256]{2,1,0:T(8,128)(2,1)} %gather_fusion, pred[128]{0:T(512)(128)(4,1)S(1)} %get-tuple-element.386, bf16[512,128,128]{2,1,0:T(8,128)(2,1)} %get-tuple-element.422, s32[]{:T(128)S(6)} %select_n.85), kind=kOutput, calls=%fused_computation.4.clone.1 | convolution fusion | flops 1082130432 | bytes 29360772 | tf_op jit(solution)/shard_map/while/body/eval_jaxpr/tab,tbf->taf/dot_general | solution.py:24
  260.1 37.9 %scatter_fusion = f32[32,128,256]{2,1,0:T(8,128)} fusion(f32[32,128,256]{2,1,0:T(8,128)} %get-tuple-element.409, s32[128]{0:T(128)S(1)} %compare_select_fusion.8, f32[128,128,256]{2,1,0:T(8,128)} %convolution_multiply_fusion.4), kind=kCustom, calls=%fused_computation.2.clone.1 | custom fusion | flops 4194304 | bytes 50332160 | tf_op jit(solution)/shard_map/while/body/eval_jaxpr/scatter-add | solution.py:28
  298.0 83.2 %reduce-scatter.3.cloned.1.call-done = f32[512,256]{1,0:T(8,128)} async-done(((f32[4096,256]{1,0:T(8,128)}), f32[512,256]{1,0:T(8,128)}) %reduce-scatter.3.cloned.1.call-update) | async-done | bytes 524304 | tf_op jit(solution)/shard_map/reduce_scatter | solution.py:52
  383.6 22.4 %copy.10 = bf16[1,1,512,128,128]{3,4,2,1,0:T(8,128)(2,1)} copy(bf16[1,1,512,128,128]{4,3,2,1,0:T(8,128)(2,1)} %bitcast.21) | data formatting | bytes 33554432 | tf_op args[5]
  406.0 31.9 %all-gather.5.cloned.1.call-done = bf16[4096,256]{1,0:T(8,128)(2,1)} async-done(((bf16[512,256]{1,0:T(8,128)(2,1)}), bf16[4096,256]{1,0:T(8,128)(2,1)}) %all-gather.5.cloned.1.call-update) | async-done | bytes 2097168 | tf_op jit(solution)/shard_map/all_gather | solution.py:55
  442.1 236.8 %while.27 = (s32[]{:T(128)}, f32[64,128,256]{2,1,0:T(8,128)}, s32[512]{0:T(512)}, bf16[512,128,128]{1,2,0:T(8,128)(2,1)}, s32[512]{0:T(512)}, /*index=5*/bf16[32...) while((s32[]{:T(128)}, f32[64,128,256]{2,1,0:T(8,128)}, ...), condition=%wide.region_6.7_spmd, body=%wide.region_4.6_spmd.sunk | while | flops 1086327040 | bytes 96478248 | solution.py:31
  449.5 12.8 %convolution_multiply_fusion.5 = f32[128,128,256]{2,1,0:T(8,128)} fusion(f32[128]{0:T(128)S(1)} %get-tuple-element.394, bf16[128,128,256]{2,1,0:T(8,128)(2,1)} %gather_fusion.1, pred[128]{0:T(512)(128)(4,1)S(1)} %get-tuple-element.396, bf16[512,128,128]{1,2,0:T(8,128)(2,1)} %get-tuple-element.455, s32[]{:T(128)S(6)} %select_n.88), kind=kOutput, calls=%fused_computation.16.clone.1 | convolution fusion | flops 1082130432 | bytes 29360772 | tf_op jit(solution)/shard_map/while/body/eval_jaxpr/tba,tbf->taf/dot_general | solution.py:24
  463.1 38.5 %scatter_fusion.1 = f32[64,128,256]{2,1,0:T(8,128)} fusion(f32[64,128,256]{2,1,0:T(8,128)} %get-tuple-element.442, s32[128]{0:T(128)S(1)} %compare_select_fusion.9, f32[128,128,256]{2,1,0:T(8,128)} %convolution_multiply_fusion.5), kind=kCustom, calls=%fused_computation.3.clone.1 | custom fusion | flops 4194304 | bytes 50332160 | tf_op jit(solution)/shard_map/while/body/eval_jaxpr/scatter-add | solution.py:28
  508.9 12.8 %convolution_multiply_fusion.5 = f32[128,128,256]{2,1,0:T(8,128)} fusion(f32[128]{0:T(128)S(1)} %get-tuple-element.394, bf16[128,128,256]{2,1,0:T(8,128)(2,1)} %gather_fusion.1, pred[128]{0:T(512)(128)(4,1)S(1)} %get-tuple-element.396, bf16[512,128,128]{1,2,0:T(8,128)(2,1)} %get-tuple-element.455, s32[]{:T(128)S(6)} %select_n.88), kind=kOutput, calls=%fused_computation.16.clone.1 | convolution fusion | flops 1082130432 | bytes 29360772 | tf_op jit(solution)/shard_map/while/body/eval_jaxpr/tba,tbf->taf/dot_general | solution.py:24
  522.5 38.1 %scatter_fusion.1 = f32[64,128,256]{2,1,0:T(8,128)} fusion(f32[64,128,256]{2,1,0:T(8,128)} %get-tuple-element.442, s32[128]{0:T(128)S(1)} %compare_select_fusion.9, f32[128,128,256]{2,1,0:T(8,128)} %convolution_multiply_fusion.5), kind=kCustom, calls=%fused_computation.3.clone.1 | custom fusion | flops 4194304 | bytes 50332160 | tf_op jit(solution)/shard_map/while/body/eval_jaxpr/scatter-add | solution.py:28
  567.9 12.8 %convolution_multiply_fusion.5 = f32[128,128,256]{2,1,0:T(8,128)} fusion(f32[128]{0:T(128)S(1)} %get-tuple-element.394, bf16[128,128,256]{2,1,0:T(8,128)(2,1)} %gather_fusion.1, pred[128]{0:T(512)(128)(4,1)S(1)} %get-tuple-element.396, bf16[512,128,128]{1,2,0:T(8,128)(2,1)} %get-tuple-element.455, s32[]{:T(128)S(6)} %select_n.88), kind=kOutput, calls=%fused_computation.16.clone.1 | convolution fusion | flops 1082130432 | bytes 29360772 | tf_op jit(solution)/shard_map/while/body/eval_jaxpr/tba,tbf->taf/dot_general | solution.py:24
  581.5 38.3 %scatter_fusion.1 = f32[64,128,256]{2,1,0:T(8,128)} fusion(f32[64,128,256]{2,1,0:T(8,128)} %get-tuple-element.442, s32[128]{0:T(128)S(1)} %compare_select_fusion.9, f32[128,128,256]{2,1,0:T(8,128)} %convolution_multiply_fusion.5), kind=kCustom, calls=%fused_computation.3.clone.1 | custom fusion | flops 4194304 | bytes 50332160 | tf_op jit(solution)/shard_map/while/body/eval_jaxpr/scatter-add | solution.py:28
  627.1 12.8 %convolution_multiply_fusion.5 = f32[128,128,256]{2,1,0:T(8,128)} fusion(f32[128]{0:T(128)S(1)} %get-tuple-element.394, bf16[128,128,256]{2,1,0:T(8,128)(2,1)} %gather_fusion.1, pred[128]{0:T(512)(128)(4,1)S(1)} %get-tuple-element.396, bf16[512,128,128]{1,2,0:T(8,128)(2,1)} %get-tuple-element.455, s32[]{:T(128)S(6)} %select_n.88), kind=kOutput, calls=%fused_computation.16.clone.1 | convolution fusion | flops 1082130432 | bytes 29360772 | tf_op jit(solution)/shard_map/while/body/eval_jaxpr/tba,tbf->taf/dot_general | solution.py:24
  640.7 38.3 %scatter_fusion.1 = f32[64,128,256]{2,1,0:T(8,128)} fusion(f32[64,128,256]{2,1,0:T(8,128)} %get-tuple-element.442, s32[128]{0:T(128)S(1)} %compare_select_fusion.9, f32[128,128,256]{2,1,0:T(8,128)} %convolution_multiply_fusion.5), kind=kCustom, calls=%fused_computation.3.clone.1 | custom fusion | flops 4194304 | bytes 50332160 | tf_op jit(solution)/shard_map/while/body/eval_jaxpr/scatter-add | solution.py:28
  679.1 71.8 %reduce-scatter.5.cloned.1.call-done = f32[512,256]{1,0:T(8,128)} async-done(((f32[8192,256]{1,0:T(8,128)}), f32[512,256]{1,0:T(8,128)}) %reduce-scatter.5.cloned.1.call-update) | async-done | bytes 524304 | tf_op jit(solution)/shard_map/reduce_scatter | solution.py:66
  752.9 119.6 %all-reduce.3.cloned.1.call-done = f32[256,256]{0,1:T(8,128)} async-done(((f32[256,256]{0,1:T(8,128)}), f32[256,256]{0,1:T(8,128)}) %all-reduce.3.cloned.1.call-update) | async-done | bytes 262160 | tf_op jit(solution)/shard_map/psum | solution.py:73
  874.6 80.4 %all-reduce.5.cloned.1.call-done = f32[256,256]{0,1:T(8,128)} async-done(((f32[256,256]{0,1:T(8,128)}), f32[256,256]{0,1:T(8,128)}) %all-reduce.5.cloned.1.call-update) | async-done | bytes 262160 | tf_op jit(solution)/shard_map/psum | solution.py:73
  (61 shorter events, 104.1 us)
Async XLA Ops:
  7.2 1.0 copy-start
  7.2 44.2 %all-gather.3.cloned.1.call-start = ((), (), s32[]{:S(2)}) async-start(), calls=%async_computation.2 | async-start | bytes 4456448 | tf_op jit(solution)/shard_map/all_gather | solution.py:48
  10.0 371.3 %reduce-scatter.3.cloned.1.call-start = ((), (), s32[]{:S(2)}) async-start(), calls=%async_computation.3 | async-start | bytes 4718592 | tf_op jit(solution)/shard_map/reduce_scatter | solution.py:52
  53.8 327.5 %copy-start.3 = (bf16[512,256]{1,0:T(8,128)(2,1)S(1)}, bf16[512,256]{1,0:T(8,128)(2,1)}, u32[]{:S(2)}) copy-start(bf16[512,256]{1,0:T(8,128)(2,1)} %param.13) | copy-start | bytes 786436
  298.0 139.9 %all-gather.5.cloned.1.call-start = ((), (), s32[]{:S(2)}) async-start(), calls=%async_computation.4 | async-start | bytes 2359296 | tf_op jit(solution)/shard_map/all_gather | solution.py:55
  383.4 367.4 %reduce-scatter.5.cloned.1.call-start = ((), (), s32[]{:S(2)}) async-start(), calls=%async_computation.5 | async-start | bytes 8912896 | tf_op jit(solution)/shard_map/reduce_scatter | solution.py:66
  437.9 4.2 copy-start.1
  679.0 193.6 %copy-start.2 = (bf16[256,256]{1,0:T(8,128)(2,1)S(1)}, bf16[256,256]{1,0:T(8,128)(2,1)}, u32[]{:S(2)}) copy-start(bf16[256,256]{1,0:T(8,128)(2,1)} %param.12) | copy-start | bytes 393220
  679.0 193.5 %all-reduce.3.cloned.1.call-start = ((), (), s32[]{:S(2)}) async-start(), calls=%async_computation.6 | async-start | bytes 524288 | tf_op jit(solution)/shard_map/psum | solution.py:73
  752.8 202.1 %all-reduce.5.cloned.1.call-start = ((), (), s32[]{:S(2)}) async-start(), calls=%async_computation.7 | async-start | bytes 524288 | tf_op jit(solution)/shard_map/psum | solution.py:73
Sparse Core Ops, SparseCore 0:
  10.3 41.0 all-gather.2
  298.1 83.1 reduce-scatter.2
  384.2 53.6 all-gather.4
  679.1 71.6 reduce-scatter.4
  753.7 118.7 all-reduce.2
  875.0 79.8 all-reduce.4
